TPU v7x, 32 devices: a whole 2x2x4 slice. The times are simulated.
32 devices in a mesh: prow: 4 (over y, x), pcol: 8 (over z, core).
Axes of the slice: x: 2, y: 2, z: 4, core: 2. Of those that a mesh axis runs over, the one named last changes fastest.
Arguments:
- matrix: float32 [4, 1024, 8, 1536], P('prow', None, 'pcol')
- pivots: int32 [256], replicated, may hold values from 256 to 4095, as said below
Outputs:
- factored: float32 [4, 1024, 8, 1536], P('prow', None, 'pcol')
Inputs may be any that keep to these rules, and one draw needn't show every extreme that they name: The 256 pivots are distinct global row indices; the values 256 and 4095 both occur.
All inputs are finite; a program needn't handle non-finite values.
Results may differ from a plain program's by a relative error of at most 0.000082.
Values sent between devices are 32-bit elements; how exact they have to be, the bound alone decides.
No kernel may reach another device: no remote copies, remote signals or barrier semaphores. Data moves between devices by JAX's collectives and lax.ppermute only.
A program may use at most 128 MiB of HBM per device.

v0:
```python
import jax
import jax.numpy as jnp
from jax import lax
from jax.sharding import PartitionSpec as P


def spread(array, axis, root):
    mine = lax.axis_index(axis) == root
    return lax.psum(jnp.where(mine, array, jnp.zeros_like(array)), axis)


def product(left, right):
    return jnp.dot(left, right, precision=lax.Precision.HIGHEST)


def eliminate(square):
    extent = square.shape[0]
    positions = jnp.arange(extent)

    def column_step(column, working):
        is_below = positions > column
        pivot_line = jnp.where(is_below, working[column, :], 0.0)
        factor_col = jnp.where(is_below, working[:, column] / working[column, column], 0.0)
        working = working - factor_col[:, None] * pivot_line[None, :]
        return jnp.where(
            is_below[:, None] & (positions == column)[None, :], factor_col[:, None], working
        )

    return lax.fori_loop(0, extent, column_step, square)


def nilpotent_inverse(strict_part):
    extent = strict_part.shape[0]
    identity = jnp.eye(extent, dtype=jnp.float32)
    result = identity - strict_part
    power = product(strict_part, strict_part)
    for level in range(3):
        result = product(result, identity + power)
        power = product(power, power)
    return result


def unit_lower_inverse(lower_tri):
    extent = lower_tri.shape[0]
    if extent <= 16:
        return nilpotent_inverse(jnp.tril(lower_tri, -1))
    midpoint = extent // 2
    first_inv = unit_lower_inverse(lower_tri[:midpoint, :midpoint])
    second_inv = unit_lower_inverse(lower_tri[midpoint:, midpoint:])
    off_block = -product(product(second_inv, lower_tri[midpoint:, :midpoint]), first_inv)
    zeros_block = jnp.zeros((midpoint, extent - midpoint), jnp.float32)
    top_part = jnp.concatenate([first_inv, zeros_block], axis=1)
    bottom_part = jnp.concatenate([off_block, second_inv], axis=1)
    return jnp.concatenate([top_part, bottom_part], axis=0)


def upper_inverse(upper_tri):
    extent = upper_tri.shape[0]
    if extent <= 16:
        diagonal = jnp.diagonal(upper_tri)
        scaled = jnp.triu(upper_tri, 1) / diagonal[:, None]
        return nilpotent_inverse(scaled) / diagonal[None, :]
    midpoint = extent // 2
    first_inv = upper_inverse(upper_tri[:midpoint, :midpoint])
    second_inv = upper_inverse(upper_tri[midpoint:, midpoint:])
    off_block = -product(product(first_inv, upper_tri[:midpoint, midpoint:]), second_inv)
    zeros_block = jnp.zeros((extent - midpoint, midpoint), jnp.float32)
    top_part = jnp.concatenate([first_inv, off_block], axis=1)
    bottom_part = jnp.concatenate([zeros_block, second_inv], axis=1)
    return jnp.concatenate([top_part, bottom_part], axis=0)


def factor(square):
    extent = square.shape[0]
    if extent <= 16:
        return eliminate(square)
    midpoint = extent // 2
    first_part = factor(square[:midpoint, :midpoint])
    upper_inv = upper_inverse(jnp.triu(first_part))
    lower_inv = unit_lower_inverse(jnp.tril(first_part, -1) + jnp.eye(midpoint, dtype=jnp.float32))
    below_left = product(square[midpoint:, :midpoint], upper_inv)
    above_right = product(lower_inv, square[:midpoint, midpoint:])
    reduced = square[midpoint:, midpoint:] - product(below_left, above_right)
    second_part = factor(reduced)
    top_part = jnp.concatenate([first_part, above_right], axis=1)
    bottom_part = jnp.concatenate([below_left, second_part], axis=1)
    return jnp.concatenate([top_part, bottom_part], axis=0)


def on_device(matrix, pivots):
    own_block = matrix[0, :, 0, :]
    rows_local = own_block.shape[0]
    panel_width = pivots.shape[0]
    row_count = lax.axis_size("prow")
    row_index = lax.axis_index("prow")
    col_index = lax.axis_index("pcol")
    local_rows = jnp.arange(rows_local, dtype=jnp.int32)
    global_rows = (
        local_rows // panel_width * row_count + row_index
    ) * panel_width + local_rows % panel_width
    owner_row = pivots // panel_width % row_count
    owner_slot = pivots // (panel_width * row_count) * panel_width + pivots % panel_width
    is_owner = owner_row == row_index
    selector = ((owner_slot[:, None] == local_rows[None, :]) & is_owner[:, None]).astype(
        jnp.float32
    )
    picked = product(selector, own_block)
    swapped_top = lax.psum(picked, "prow")
    old_top = spread(own_block[:panel_width], "prow", 0)
    matches = (global_rows[:, None] == pivots[None, :]).astype(jnp.float32)
    is_target = jnp.sum(matches, axis=1) > 0.5
    swapped = jnp.where(is_target[:, None], product(matches, old_top), own_block)
    swapped = swapped.at[:panel_width].set(
        jnp.where(row_index == 0, swapped_top, swapped[:panel_width])
    )
    identity = jnp.eye(panel_width, dtype=jnp.float32)
    packed = factor(jnp.where(col_index == 0, swapped_top[:, :panel_width], identity))
    upper_inv = upper_inverse(jnp.triu(packed))
    lower_left = product(swapped[:, :panel_width], upper_inv)
    left_all, packed_all = (spread(lower_left, "pcol", 0), spread(packed, "pcol", 0))
    lower_inv = unit_lower_inverse(jnp.tril(packed_all, -1) + identity)
    own_upper = product(lower_inv, swapped[:panel_width])
    upper_right = spread(own_upper, "prow", 0)
    trailing = swapped - product(left_all, upper_right)
    first_cols = jnp.where(col_index == 0, left_all, trailing[:, :panel_width])
    result = trailing.at[:, :panel_width].set(first_cols)
    top_block = upper_right.at[:, :panel_width].set(
        jnp.where(col_index == 0, packed_all, upper_right[:, :panel_width])
    )
    result = result.at[:panel_width].set(jnp.where(row_index == 0, top_block, result[:panel_width]))
    return result[None, :, None, :]


def solution(mesh):
    in_specs = (P("prow", None, "pcol", None), P())
    out_specs = P("prow", None, "pcol", None)
    return jax.shard_map(
        on_device, mesh=mesh, in_specs=in_specs, out_specs=out_specs, check_vma=False
    )
```

profile of v0, /device:TPU:0, one launch (start us, length us, event | category | flops | bytes accessed | tf_op | source)
XLA Modules:
  0.0 852.0 jit_solution(1302605597566347731)
XLA Ops:
  7.9 2.9 broadcast_select_fusion
  10.9 1.2 copy.216
  12.1 4.6 fusion.64
  17.8 89.2 %all-reduce.74.cloned.1.call-done = (f32[256,1536]{1,0:T(8,128)}, f32[256,1536]{1,0:T(8,128)}) async-done(((f32[256,1536]{1,0:T(8,128)}, f32[256,1536]{1,0:T(8,128)}), (f32[256,1536]{1,0:T(8,128)}, f32[256,1536]{1,0:T(8,128)})) %all-reduce.74.cloned.1.call-update) | async-done | bytes 3145744 | tf_op jit(solution)/shard_map/psum | solution.py:9
  107.0 1.0 convert_select_fusion
  108.0 22.7 %while.244 = (s32[]{:T(128)}, f32[16,16]{0,1:T(8,128)S(1)}, s32[]{:T(128)}) while((s32[]{:T(128)}, f32[16,16]{0,1:T(8,128)S(1)}, s32[]{:T(128)}) %tuple.621), condition=%wide.region_4.5_spmd.clone.clone, body=%wide.region_3.4_spmd.clone.clone.sunk | while | flops 1138 | bytes 6665 | solution.py:29
  134.0 22.8 %while.245 = (s32[]{:T(128)}, f32[16,16]{0,1:T(8,128)S(1)}, s32[]{:T(128)}) while((s32[]{:T(128)}, f32[16,16]{0,1:T(8,128)S(1)}, s32[]{:T(128)}) %tuple.624), condition=%wide.region_6.7_spmd.clone.clone, body=%wide.region_5.6_spmd.clone.clone.sunk | while | flops 1138 | bytes 6665 | solution.py:29
  163.5 22.7 %while.246 = (s32[]{:T(128)}, f32[16,16]{0,1:T(8,128)S(1)}, s32[]{:T(128)}) while((s32[]{:T(128)}, f32[16,16]{0,1:T(8,128)S(1)}, s32[]{:T(128)}) %tuple.627), condition=%wide.region_8.9_spmd.clone.clone, body=%wide.region_7.8_spmd.clone.clone.sunk | while | flops 1138 | bytes 6665 | solution.py:29
  189.4 22.8 %while.247 = (s32[]{:T(128)}, f32[16,16]{0,1:T(8,128)S(1)}, s32[]{:T(128)}) while((s32[]{:T(128)}, f32[16,16]{0,1:T(8,128)S(1)}, s32[]{:T(128)}) %tuple.630), condition=%wide.region_10.11_spmd.clone.clone, body=%wide.region_9.10_spmd.clone.clone.sunk | while | flops 1138 | bytes 6665 | solution.py:29
  226.0 22.7 %while.248 = (s32[]{:T(128)}, f32[16,16]{0,1:T(8,128)S(1)}, s32[]{:T(128)}) while((s32[]{:T(128)}, f32[16,16]{0,1:T(8,128)S(1)}, s32[]{:T(128)}) %tuple.633), condition=%wide.region_12.13_spmd.clone.clone, body=%wide.region_11.12_spmd.clone.clone.sunk | while | flops 1138 | bytes 6665 | solution.py:29
  252.0 22.8 %while.249 = (s32[]{:T(128)}, f32[16,16]{0,1:T(8,128)S(1)}, s32[]{:T(128)}) while((s32[]{:T(128)}, f32[16,16]{0,1:T(8,128)S(1)}, s32[]{:T(128)}) %tuple.636), condition=%wide.region_14.15_spmd.clone.clone, body=%wide.region_13.14_spmd.clone.clone.sunk | while | flops 1138 | bytes 6665 | solution.py:29
  281.4 22.7 %while.250 = (s32[]{:T(128)}, f32[16,16]{0,1:T(8,128)S(1)}, s32[]{:T(128)}) while((s32[]{:T(128)}, f32[16,16]{0,1:T(8,128)S(1)}, s32[]{:T(128)}) %tuple.639), condition=%wide.region_16.17_spmd.clone.clone, body=%wide.region_15.16_spmd.clone.clone.sunk | while | flops 1138 | bytes 6665 | solution.py:29
  307.4 22.9 %while.251 = (s32[]{:T(128)}, f32[16,16]{0,1:T(8,128)S(1)}, s32[]{:T(128)}) while((s32[]{:T(128)}, f32[16,16]{0,1:T(8,128)S(1)}, s32[]{:T(128)}) %tuple.642), condition=%wide.region_18.19_spmd.clone.clone, body=%wide.region_17.18_spmd.clone.clone.sunk | while | flops 1138 | bytes 6665 | solution.py:29
  331.4 1.0 fusion.1087
  334.1 1.0 fusion.1086
  336.8 1.0 fusion.1085
  339.5 1.0 fusion.1084
  342.2 1.0 fusion.1083
  344.9 1.0 fusion.1082
  347.5 1.0 fusion.1081
  350.2 1.0 fusion.1080
  370.1 22.7 %while.252 = (s32[]{:T(128)}, f32[16,16]{0,1:T(8,128)S(1)}, s32[]{:T(128)}) while((s32[]{:T(128)}, f32[16,16]{0,1:T(8,128)S(1)}, s32[]{:T(128)}) %tuple.645), condition=%wide.region_20.21_spmd.clone.clone, body=%wide.region_19.20_spmd.clone.clone.sunk | while | flops 1138 | bytes 6665 | solution.py:29
  396.1 22.8 %while.253 = (s32[]{:T(128)}, f32[16,16]{0,1:T(8,128)S(1)}, s32[]{:T(128)}) while((s32[]{:T(128)}, f32[16,16]{0,1:T(8,128)S(1)}, s32[]{:T(128)}) %tuple.648), condition=%wide.region_22.23_spmd.clone.clone, body=%wide.region_21.22_spmd.clone.clone.sunk | while | flops 1138 | bytes 6665 | solution.py:29
  425.6 22.7 %while.254 = (s32[]{:T(128)}, f32[16,16]{0,1:T(8,128)S(1)}, s32[]{:T(128)}) while((s32[]{:T(128)}, f32[16,16]{0,1:T(8,128)S(1)}, s32[]{:T(128)}) %tuple.651), condition=%wide.region_24.25_spmd.clone.clone, body=%wide.region_23.24_spmd.clone.clone.sunk | while | flops 1138 | bytes 6665 | solution.py:29
  451.5 22.8 %while.255 = (s32[]{:T(128)}, f32[16,16]{0,1:T(8,128)S(1)}, s32[]{:T(128)}) while((s32[]{:T(128)}, f32[16,16]{0,1:T(8,128)S(1)}, s32[]{:T(128)}) %tuple.654), condition=%wide.region_26.27_spmd.clone.clone, body=%wide.region_25.26_spmd.clone.clone.sunk | while | flops 1138 | bytes 6665 | solution.py:29
  488.1 22.7 %while.256 = (s32[]{:T(128)}, f32[16,16]{0,1:T(8,128)S(1)}, s32[]{:T(128)}) while((s32[]{:T(128)}, f32[16,16]{0,1:T(8,128)S(1)}, s32[]{:T(128)}) %tuple.657), condition=%wide.region_28.29_spmd.clone.clone, body=%wide.region_27.28_spmd.clone.clone.sunk | while | flops 1138 | bytes 6665 | solution.py:29
  514.1 22.9 %while.257 = (s32[]{:T(128)}, f32[16,16]{0,1:T(8,128)S(1)}, s32[]{:T(128)}) while((s32[]{:T(128)}, f32[16,16]{0,1:T(8,128)S(1)}, s32[]{:T(128)}) %tuple.660), condition=%wide.region_30.31_spmd.clone.clone, body=%wide.region_29.30_spmd.clone.clone.sunk | while | flops 1138 | bytes 6665 | solution.py:29
  543.8 22.7 %while.258 = (s32[]{:T(128)}, f32[16,16]{0,1:T(8,128)S(1)}, s32[]{:T(128)}) while((s32[]{:T(128)}, f32[16,16]{0,1:T(8,128)S(1)}, s32[]{:T(128)}) %tuple.663), condition=%wide.region_32.33_spmd.clone.clone, body=%wide.region_31.32_spmd.clone.clone.sunk | while | flops 1138 | bytes 6665 | solution.py:29
  569.9 22.8 %while.259 = (s32[]{:T(128)}, f32[16,16]{0,1:T(8,128)S(1)}, s32[]{:T(128)}) while((s32[]{:T(128)}, f32[16,16]{0,1:T(8,128)S(1)}, s32[]{:T(128)}) %tuple.666), condition=%wide.region_34.35_spmd.clone.clone, body=%wide.region_33.34_spmd.clone.clone.sunk | while | flops 1138 | bytes 6665 | solution.py:29
  594.6 1.0 fusion.1115
  597.3 1.0 fusion.1114
  605.3 1.0 fusion.1111
  608.0 1.0 fusion.1110
  610.7 1.0 fusion.1109
  613.4 1.0 fusion.1108
  618.8 1.0 fusion.1106
  624.2 1.0 fusion.1104
  629.6 1.0 fusion.1102
  635.0 1.0 fusion.1100
  637.0 6.6 bitcast_select_fusion.32
  644.1 2.2 copy-done.1
  660.1 2.1 convolution_select_fusion.1
  662.2 60.4 %all-reduce.72.cloned.1.call-done = (f32[1024,256]{1,0:T(8,128)}, f32[256,256]{1,0:T(8,128)}) async-done(((f32[1024,256]{1,0:T(8,128)}, f32[256,256]{1,0:T(8,128)}), (f32[1024,256]{1,0:T(8,128)}, f32[256,256]{1,0:T(8,128)})) %all-reduce.72.cloned.1.call-update) | async-done | bytes 1310736 | tf_op jit(solution)/shard_map/psum | solution.py:9
  722.6 1.0 convert_add_fusion.296
  745.1 4.2 convolution_select_fusion
  750.3 59.1 %all-reduce.70.cloned.1.call-done = f32[256,1536]{1,0:T(8,128)} async-done(((f32[256,1536]{1,0:T(8,128)}), f32[256,1536]{1,0:T(8,128)}) %all-reduce.70.cloned.1.call-update) | async-done | bytes 1572880 | tf_op jit(solution)/shard_map/psum | solution.py:9
  809.4 8.2 convolution_subtract_fusion
  820.9 24.1 %copy.205 = f32[1,1024,1,1536]{3,2,1,0:T(1,128)} copy(f32[1,1024,1,1536]{3,1,2,0:T(8,128)S(1)} %fusion.68) | data formatting | bytes 12582912 | tf_op jit(solution)/shard_map/scatter | solution.py:130
  (2482 shorter events, 548.1 us)
Async XLA Ops:
  6.5 100.4 %all-reduce.74.cloned.1.call-start = ((), (), s32[]{:S(2)}) async-start(), calls=%async_computation.2 | async-start | bytes 6291456 | tf_op jit(solution)/shard_map/psum | solution.py:9
  7.9 4.2 copy-start.2
  16.7 0.7 copy-start.12
  16.7 705.8 %all-reduce.72.cloned.1.call-start = ((), (), s32[]{:S(2)}) async-start(), calls=%async_computation.1 | async-start | bytes 2621440 | tf_op jit(solution)/shard_map/psum | solution.py:9
  330.6 0.8 copy-start.10
  344.2 13.2 %copy-start.11 = (f32[128,128]{1,0:T(8,128)S(1)}, f32[128,128]{1,0:T(8,128)}, u32[]{:S(2)}) copy-start(f32[128,128]{1,0:T(8,128)} %copy-done.10) | copy-start | bytes 196612
  593.8 0.8 copy-start.6
  624.2 12.9 %copy-start.8 = (f32[256,1536]{1,0:T(8,128)S(1)}, f32[256,1536]{1,0:T(8,128)}, u32[]{:S(2)}) copy-start(f32[256,1536]{1,0:T(8,128)} %get-tuple-element.1559) | copy-start | bytes 4718596
  643.6 2.7 copy-start.1
  643.6 2.7 copy-start.4
  646.3 1.1 copy-start.7
  646.7 13.4 %copy-start = (f32[1024,1536]{1,0:T(8,128)}, f32[1024,1536]{1,0:T(8,128)S(1)}, u32[]{:S(2)}) copy-start(f32[1024,1536]{1,0:T(8,128)S(1)} %fusion.75) | copy-start | bytes 18874372
  662.2 147.2 %all-reduce.70.cloned.1.call-start = ((), (), s32[]{:S(2)}) async-start(), calls=%async_computation | async-start | bytes 3145728 | tf_op jit(solution)/shard_map/psum | solution.py:9
  749.3 60.1 %copy-start.5 = (f32[1024,256]{1,0:T(8,128)S(1)}, f32[1024,256]{1,0:T(8,128)}, u32[]{:S(2)}) copy-start(f32[1024,256]{1,0:T(8,128)} %get-tuple-element.1557) | copy-start | bytes 3145732
  818.5 1.4 copy-start.3
  818.5 1.4 copy-start.9
Sparse Core Ops, SparseCore 0:
  16.8 90.0 all-reduce.73
  662.3 60.2 all-reduce.71
  749.4 59.8 all-reduce.69
where the time goes:
time: 861 us; the launch traced here: 852 us
  local copies, waits for them, and re-layouts  235 us (27%)
  waiting for transfers between devices  209 us (24%)
  other arithmetic  205 us (24%)
  matrix products  183 us (21%)
  between operations  15 us (2%)
    psum x3, waiting for transfers between devices, spread(): return lax.psum(jnp.where(mine, array, jnp.zeros_like(array)), axis)  209 us
    dot_general x754, matrix products, product(): return jnp.dot(left, right, precision=lax.Precision.HIGHEST)  183 us
    broadcast_in_dim x256, other arithmetic, column_step(): jnp.where(is_below[:, None] & (positions == column)[None, :], factor_col[...  167 us
    dynamic_slice x256, local copies, waits for them, and re-layouts, column_step(): working[column, column]  150 us
    gather x48, local copies, waits for them, and re-layouts, upper_inverse(): diagonal = jnp.diagonal(upper_tri)  32.2 us
    scatter x1, local copies, waits for them, and re-layouts, on_device(): result.at[:panel_width]  24.1 us
    select_n x256, other arithmetic, column_step(): jnp.where(is_below[:, None] & (positions == column)[None, :], factor_col[...  19.4 us
    while x256, local copies, waits for them, and re-layouts  18.7 us
  transfers between devices with their start and end apart: 3, of which 3 were waited for; matrix products, arithmetic and copies ran while one was open for 0% of the time, Pallas kernels for 0%

commit v1 on v0

--- a/solution.py
+++ b/solution.py
@@ -6,7 +6,7 @@
 
 def spread(array, axis, root):
     mine = lax.axis_index(axis) == root
-    return lax.psum(jnp.where(mine, array, jnp.zeros_like(array)), axis)
+    return jnp.sum(lax.all_gather(jnp.where(mine, array, jnp.zeros_like(array)), axis), axis=0)
 
 
 def product(left, right):

time: 861 us -> 896 us (1.041)
  other arithmetic: 205 us -> 219 us
    all_gather x0 -> x4, waiting for transfers between devices: none -> 153 us  [spread(): lax.all_gather(jnp.where(mine, array, jnp.zeros_like(array)), axis)]
    psum x3 -> x1, waiting for transfers between devices: 209 us -> 63.6 us  [on_device(): swapped_top = lax.psum(picked, 'prow')]
    reduce_sum x0 -> x4, other arithmetic: none -> 13.1 us  [spread(): jnp.sum(lax.all_gather(jnp.where(mine, array, jnp.zeros_like(array)), axi...]
  transfers between devices with their start and end apart: 3 -> 5, of which waited for: 3 -> 4; matrix products, arithmetic and copies ran while one was open for 0% -> 11% of each run, Pallas kernels for 0% -> 0%
where the time goes in v1:
time: 896 us; the launch traced here: 883 us
  local copies, waits for them, and re-layouts  240 us (27%)
  other arithmetic  219 us (24%)
  waiting for transfers between devices  216 us (24%)
  matrix products  187 us (21%)
  between operations  15 us (2%)
    dot_general x754, matrix products, product(): return jnp.dot(left, right, precision=lax.Precision.HIGHEST)  187 us
    broadcast_in_dim x256, other arithmetic, column_step(): jnp.where(is_below[:, None] & (positions == column)[None, :], factor_col[...  167 us
    all_gather x4, waiting for transfers between devices, spread(): lax.all_gather(jnp.where(mine, array, jnp.zeros_like(array)), axis)  153 us
    dynamic_slice x256, local copies, waits for them, and re-layouts, column_step(): working[column, column]  151 us
    psum x1, waiting for transfers between devices, on_device(): swapped_top = lax.psum(picked, 'prow')  63.6 us
    gather x48, local copies, waits for them, and re-layouts, upper_inverse(): diagonal = jnp.diagonal(upper_tri)  33.7 us
    scatter x1, local copies, waits for them, and re-layouts, on_device(): result.at[:panel_width]  24.1 us
    select_n x256, other arithmetic, column_step(): jnp.where(is_below[:, None] & (positions == column)[None, :], factor_col[...  19.9 us
  transfers between devices with their start and end apart: 5, of which 4 were waited for; matrix products, arithmetic and copies ran while one was open for 11% of the time, Pallas kernels for 0%

profile of v1, /device:TPU:0, one launch (start us, length us, event | category | flops | bytes accessed | tf_op | source)
XLA Modules:
  0.0 882.7 jit_solution(12192244260481766028)
XLA Ops:
  7.9 7.4 fusion.64
  15.4 63.6 %all-reduce.66.cloned.1.call-done = f32[256,1536]{1,0:T(8,128)} async-done(((f32[256,1536]{1,0:T(8,128)}), f32[256,1536]{1,0:T(8,128)}) %all-reduce.66.cloned.1.call-update) | async-done | bytes 1572880 | tf_op jit(solution)/shard_map/psum | solution.py:108
  79.0 1.0 convert_select_fusion
  80.1 22.7 %while.244 = (s32[]{:T(128)}, f32[16,16]{0,1:T(8,128)S(1)}, s32[]{:T(128)}) while((s32[]{:T(128)}, f32[16,16]{0,1:T(8,128)S(1)}, s32[]{:T(128)}) %tuple.636), condition=%wide.region_4.5_spmd.clone.clone, body=%wide.region_3.4_spmd.clone.clone.sunk | while | flops 1138 | bytes 6665 | solution.py:29
  106.1 22.7 %while.245 = (s32[]{:T(128)}, f32[16,16]{0,1:T(8,128)S(1)}, s32[]{:T(128)}) while((s32[]{:T(128)}, f32[16,16]{0,1:T(8,128)S(1)}, s32[]{:T(128)}) %tuple.639), condition=%wide.region_6.7_spmd.clone.clone, body=%wide.region_5.6_spmd.clone.clone.sunk | while | flops 1138 | bytes 6665 | solution.py:29
  135.6 22.7 %while.246 = (s32[]{:T(128)}, f32[16,16]{0,1:T(8,128)S(1)}, s32[]{:T(128)}) while((s32[]{:T(128)}, f32[16,16]{0,1:T(8,128)S(1)}, s32[]{:T(128)}) %tuple.642), condition=%wide.region_8.9_spmd.clone.clone, body=%wide.region_7.8_spmd.clone.clone.sunk | while | flops 1138 | bytes 6665 | solution.py:29
  161.5 22.7 %while.247 = (s32[]{:T(128)}, f32[16,16]{0,1:T(8,128)S(1)}, s32[]{:T(128)}) while((s32[]{:T(128)}, f32[16,16]{0,1:T(8,128)S(1)}, s32[]{:T(128)}) %tuple.645), condition=%wide.region_10.11_spmd.clone.clone, body=%wide.region_9.10_spmd.clone.clone.sunk | while | flops 1138 | bytes 6665 | solution.py:29
  198.1 22.7 %while.248 = (s32[]{:T(128)}, f32[16,16]{0,1:T(8,128)S(1)}, s32[]{:T(128)}) while((s32[]{:T(128)}, f32[16,16]{0,1:T(8,128)S(1)}, s32[]{:T(128)}) %tuple.648), condition=%wide.region_12.13_spmd.clone.clone, body=%wide.region_11.12_spmd.clone.clone.sunk | while | flops 1138 | bytes 6665 | solution.py:29
  224.1 22.7 %while.249 = (s32[]{:T(128)}, f32[16,16]{0,1:T(8,128)S(1)}, s32[]{:T(128)}) while((s32[]{:T(128)}, f32[16,16]{0,1:T(8,128)S(1)}, s32[]{:T(128)}) %tuple.651), condition=%wide.region_14.15_spmd.clone.clone, body=%wide.region_13.14_spmd.clone.clone.sunk | while | flops 1138 | bytes 6665 | solution.py:29
  253.6 22.7 %while.250 = (s32[]{:T(128)}, f32[16,16]{0,1:T(8,128)S(1)}, s32[]{:T(128)}) while((s32[]{:T(128)}, f32[16,16]{0,1:T(8,128)S(1)}, s32[]{:T(128)}) %tuple.654), condition=%wide.region_16.17_spmd.clone.clone, body=%wide.region_15.16_spmd.clone.clone.sunk | while | flops 1138 | bytes 6665 | solution.py:29
  279.5 22.9 %while.251 = (s32[]{:T(128)}, f32[16,16]{0,1:T(8,128)S(1)}, s32[]{:T(128)}) while((s32[]{:T(128)}, f32[16,16]{0,1:T(8,128)S(1)}, s32[]{:T(128)}) %tuple.657), condition=%wide.region_18.19_spmd.clone.clone, body=%wide.region_17.18_spmd.clone.clone.sunk | while | flops 1138 | bytes 6665 | solution.py:29
  307.9 1.0 fusion.1080
  310.6 1.0 fusion.1081
  316.0 1.0 fusion.1083
  318.7 1.0 fusion.1084
  326.8 1.0 fusion.1079
  342.4 22.7 %while.252 = (s32[]{:T(128)}, f32[16,16]{0,1:T(8,128)S(1)}, s32[]{:T(128)}) while((s32[]{:T(128)}, f32[16,16]{0,1:T(8,128)S(1)}, s32[]{:T(128)}) %tuple.660), condition=%wide.region_20.21_spmd.clone.clone, body=%wide.region_19.20_spmd.clone.clone.sunk | while | flops 1138 | bytes 6665 | solution.py:29
  368.4 22.7 %while.253 = (s32[]{:T(128)}, f32[16,16]{0,1:T(8,128)S(1)}, s32[]{:T(128)}) while((s32[]{:T(128)}, f32[16,16]{0,1:T(8,128)S(1)}, s32[]{:T(128)}) %tuple.663), condition=%wide.region_22.23_spmd.clone.clone, body=%wide.region_21.22_spmd.clone.clone.sunk | while | flops 1138 | bytes 6665 | solution.py:29
  397.9 22.7 %while.254 = (s32[]{:T(128)}, f32[16,16]{0,1:T(8,128)S(1)}, s32[]{:T(128)}) while((s32[]{:T(128)}, f32[16,16]{0,1:T(8,128)S(1)}, s32[]{:T(128)}) %tuple.666), condition=%wide.region_24.25_spmd.clone.clone, body=%wide.region_23.24_spmd.clone.clone.sunk | while | flops 1138 | bytes 6665 | solution.py:29
  423.9 22.7 %while.255 = (s32[]{:T(128)}, f32[16,16]{0,1:T(8,128)S(1)}, s32[]{:T(128)}) while((s32[]{:T(128)}, f32[16,16]{0,1:T(8,128)S(1)}, s32[]{:T(128)}) %tuple.669), condition=%wide.region_26.27_spmd.clone.clone, body=%wide.region_25.26_spmd.clone.clone.sunk | while | flops 1138 | bytes 6665 | solution.py:29
  460.4 22.7 %while.256 = (s32[]{:T(128)}, f32[16,16]{0,1:T(8,128)S(1)}, s32[]{:T(128)}) while((s32[]{:T(128)}, f32[16,16]{0,1:T(8,128)S(1)}, s32[]{:T(128)}) %tuple.672), condition=%wide.region_28.29_spmd.clone.clone, body=%wide.region_27.28_spmd.clone.clone.sunk | while | flops 1138 | bytes 6665 | solution.py:29
  486.4 22.9 %while.257 = (s32[]{:T(128)}, f32[16,16]{0,1:T(8,128)S(1)}, s32[]{:T(128)}) while((s32[]{:T(128)}, f32[16,16]{0,1:T(8,128)S(1)}, s32[]{:T(128)}) %tuple.675), condition=%wide.region_30.31_spmd.clone.clone, body=%wide.region_29.30_spmd.clone.clone.sunk | while | flops 1138 | bytes 6665 | solution.py:29
  516.1 22.7 %while.258 = (s32[]{:T(128)}, f32[16,16]{0,1:T(8,128)S(1)}, s32[]{:T(128)}) while((s32[]{:T(128)}, f32[16,16]{0,1:T(8,128)S(1)}, s32[]{:T(128)}) %tuple.678), condition=%wide.region_32.33_spmd.clone.clone, body=%wide.region_31.32_spmd.clone.clone.sunk | while | flops 1138 | bytes 6665 | solution.py:29
  542.0 22.7 %while.259 = (s32[]{:T(128)}, f32[16,16]{0,1:T(8,128)S(1)}, s32[]{:T(128)}) while((s32[]{:T(128)}, f32[16,16]{0,1:T(8,128)S(1)}, s32[]{:T(128)}) %tuple.681), condition=%wide.region_34.35_spmd.clone.clone, body=%wide.region_33.34_spmd.clone.clone.sunk | while | flops 1138 | bytes 6665 | solution.py:29
  566.0 1.4 slice-done
  567.4 1.3 copy_select_fusion
  584.8 1.0 fusion.1105
  590.2 1.0 fusion.1108
  595.6 1.0 fusion.1110
  601.0 1.0 fusion.1113
  605.7 1.2 gather_fusion.32
  606.9 1.2 gather_fusion.44
  608.1 1.2 gather_fusion.40
  626.5 1.8 reduce_sum.48
  650.6 17.0 %all-gather.10.cloned.1.call-done = f32[4,256,1,1536]{3,1,2,0:T(8,128)} async-done(((f32[1,256,1,1536]{3,1,2,0:T(8,128)}), f32[4,256,1,1536]{3,1,2,0:T(8,128)}) %all-gather.10.cloned.1.call-update) | async-done | bytes 6291472 | tf_op jit(solution)/shard_map/all_gather | solution.py:9
  667.6 3.6 reduce_sum.46
  671.3 6.7 bitcast_select_fusion.32
  678.0 2.7 copy-done
  680.7 2.6 convolution_select_fusion
  691.1 3.1 fusion.75
  694.2 3.3 convolution_select_fusion.1
  698.4 55.5 %all-gather.14.cloned.1.call-done = f32[1024,1536]{1,0:T(8,128)} async-done(((f32[256,1536]{1,0:T(8,128)}), f32[1024,1536]{1,0:T(8,128)}) %all-gather.14.cloned.1.call-update) | async-done | bytes 6291472 | tf_op jit(solution)/shard_map/all_gather | solution.py:9
  753.9 3.6 reduce_sum.49
  757.6 80.0 %all-gather.12.cloned.1.call-done = f32[8192,256]{1,0:T(8,128)} async-done(((f32[1024,256]{1,0:T(8,128)}), f32[8192,256]{1,0:T(8,128)}) %all-gather.12.cloned.1.call-update) | async-done | bytes 8388624 | tf_op jit(solution)/shard_map/all_gather | solution.py:9
  837.6 4.1 reduce_sum.47
  841.7 7.8 convolution_subtract_fusion
  849.5 1.0 fusion.71
  851.9 24.1 %copy.276 = f32[1,1024,1,1536]{3,2,1,0:T(1,128)} copy(f32[1,1024,1,1536]{3,1,2,0:T(8,128)S(1)} %fusion.68) | data formatting | bytes 12582912 | tf_op jit(solution)/shard_map/scatter | solution.py:130
  (2566 shorter events, 559.2 us)
Async XLA Ops:
  6.5 72.5 %all-reduce.66.cloned.1.call-start = ((), (), s32[]{:S(2)}) async-start(), calls=%async_computation | async-start | bytes 3145728 | tf_op jit(solution)/shard_map/psum | solution.py:108
  15.3 611.2 %all-gather.8.cloned.1.call-start = ((), (), s32[]{:S(2)}) async-start(), calls=%async_computation.1 | async-start | bytes 2359296 | tf_op jit(solution)/shard_map/all_gather | solution.py:9
  307.1 0.8 copy-start.4
  325.1 13.0 %copy-start.5 = (f32[128,128]{1,0:T(8,128)S(1)}, f32[128,128]{1,0:T(8,128)}, u32[]{:S(2)}) copy-start(f32[128,128]{1,0:T(8,128)} %copy-done.4) | copy-start | bytes 196612
  565.9 101.7 %all-gather.10.cloned.1.call-start = ((), (), s32[]{:S(2)}) async-start(), calls=%async_computation.2 | async-start | bytes 7864320 | tf_op jit(solution)/shard_map/all_gather | solution.py:9
  566.0 1.4 slice-start
  568.7 185.2 %all-gather.14.cloned.1.call-start = ((), (), s32[]{:S(2)}) async-start(), calls=%async_computation.4 | async-start | bytes 7864320 | tf_op jit(solution)/shard_map/all_gather | solution.py:9
  570.5 0.8 copy-start.2
  609.7 1.8 copy-start.38
  611.7 16.5 %copy-start.29 = (f32[16,32]{1,0:T(8,128)}, f32[16,32]{1,0:T(8,128)S(1)}, u32[]{:S(2)}) copy-start(f32[16,32]{1,0:T(8,128)S(1)} %concatenate.941) | copy-start | bytes 6148
  612.7 2.7 copy-start.40
  614.3 14.0 %copy-start.42 = (f32[16,16]{1,0:T(8,128)}, f32[16,16]{1,0:T(8,128)S(1)}, u32[]{:S(2)}) copy-start(f32[16,16]{1,0:T(8,128)S(1)} %convolution_divide_fusion.2) | copy-start | bytes 3076
  615.7 12.7 %copy-start.33 = (f32[16,16]{1,0:T(8,128)}, f32[16,16]{1,0:T(8,128)S(1)}, u32[]{:S(2)}) copy-start(f32[16,16]{1,0:T(8,128)S(1)} %convolution_divide_fusion.1) | copy-start | bytes 3076
  618.0 4.7 copy-start.18
  619.4 6.4 copy-start.22
  619.5 5.3 copy-start.25
  620.6 5.2 copy-start.27
  622.0 1.4 copy-start.20
  636.0 13.4 %copy-start.13 = (f32[16,32]{1,0:T(8,128)}, f32[16,32]{1,0:T(8,128)S(1)}, u32[]{:S(2)}) copy-start(f32[16,32]{1,0:T(8,128)S(1)} %concatenate.1015) | copy-start | bytes 6148
  642.3 7.4 copy-start.10
  648.6 1.1 copy-start.15
  650.6 20.7 %copy-start.45 = (s32[256]{0:T(256)S(1)}, s32[256]{0:T(256)}, u32[]{:S(2)}) copy-start(s32[256]{0:T(256)} %param.43) | copy-start | bytes 3076
  671.2 9.5 %copy-start.1 = (f32[256,1536]{1,0:T(8,128)S(1)}, f32[256,1536]{1,0:T(8,128)}, u32[]{:S(2)}) copy-start(f32[256,1536]{1,0:T(8,128)} %all-reduce.66.cloned.1.call-done) | copy-start | bytes 4718596
  671.2 9.5 %copy-start.6 = (f32[128,128]{1,0:T(8,128)S(1)}, f32[128,128]{1,0:T(8,128)}, u32[]{:S(2)}) copy-start(f32[128,128]{1,0:T(8,128)} %convolution_negate_fusion) | copy-start | bytes 196612
  671.3 9.5 %copy-start.8 = (f32[32,32]{1,0:T(8,128)S(1)}, f32[32,32]{1,0:T(8,128)}, u32[]{:S(2)}) copy-start(f32[32,32]{1,0:T(8,128)} %copy-done.7) | copy-start | bytes 12292
  671.3 9.5 %copy-start.11 = (f32[32,64]{1,0:T(8,128)S(1)}, f32[32,64]{1,0:T(8,128)}, u32[]{:S(2)}) copy-start(f32[32,64]{1,0:T(8,128)} %copy-done.10) | copy-start | bytes 24580
  671.3 9.5 %copy-start.14 = (f32[16,32]{1,0:T(8,128)S(1)}, f32[16,32]{1,0:T(8,128)}, u32[]{:S(2)}) copy-start(f32[16,32]{1,0:T(8,128)} %copy-done.13) | copy-start | bytes 6148
  671.3 9.5 %copy-start.16 = (f32[16,16]{1,0:T(8,128)S(1)}, f32[16,16]{1,0:T(8,128)}, u32[]{:S(2)}) copy-start(f32[16,16]{1,0:T(8,128)} %copy-done.15) | copy-start | bytes 3076
  678.0 2.7 copy-start
  683.4 0.8 copy-start.32
  683.4 0.9 copy-start.34
  683.4 0.9 copy-start.36
  683.4 0.9 copy-start.37
  683.4 1.0 copy-start.3
  683.4 1.0 copy-start.48
  683.4 2.2 copy-start.43
  683.5 2.3 copy-start.31
  683.5 2.8 copy-start.47
  683.5 4.0 copy-start.41
  683.5 4.1 copy-start.24
  683.5 4.3 copy-start.19
  683.5 4.5 copy-start.17
  683.5 5.0 copy-start.46
  683.5 6.1 copy-start.39
  683.5 6.3 copy-start.12
  683.5 6.5 copy-start.21
  683.6 6.6 copy-start.9
  683.6 154.0 %all-gather.12.cloned.1.call-start = ((), (), s32[]{:S(2)}) async-start(), calls=%async_computation.3 | async-start | bytes 9437184 | tf_op jit(solution)/shard_map/all_gather | solution.py:9
  (7 other events, 4.9 us)
Sparse Core Ops, SparseCore 0:
  15.4 63.5 all-reduce.65
  566.0 29.1 all-gather.7
  597.3 70.2 all-gather.9
  683.7 70.1 all-gather.13
  755.5 82.0 all-gather.11
